TPU v7x, 32 devices: a whole 2x2x4 slice. The times are simulated.
32 devices in a mesh: groups: 2 (over x), att: 8 (over z, y), exp: 2 (over core).
Axes of the slice: x: 2, y: 2, z: 4, core: 2. Of those that a mesh axis runs over, the one named last changes fastest.
Arguments:
- query: bfloat16 [2048, 2048], P(('groups', 'att'), 'exp'), parts along dimension 0, may hold values from -9 to 9
- new_key: bfloat16 [2048, 256], P(('groups', 'att'), 'exp'), parts along dimension 0, may hold values from -6 to 6
- new_value: bfloat16 [2048, 256], P(('groups', 'att'), 'exp'), parts along dimension 0, may hold values from -6 to 6
- cache_keys: bfloat16 [2048, 64, 256], P(('groups', 'att'), None, 'exp'), parts along dimension 0, may hold values from -9 to 9
- cache_values: bfloat16 [2048, 64, 256], P(('groups', 'att'), None, 'exp'), parts along dimension 0, may hold values from -6 to 6
- lengths: int32 [2048], P(('groups', 'att')), parts along dimension 0, may hold values from 2 to 64, as said below
- out_proj: bfloat16 [2048, 2880], P('exp'), may hold values from -0.125 to 0.125
- residual: bfloat16 [2048, 2880], P(('groups', 'att', 'exp')), parts along dimension 0, may hold values from -6 to 6
- norm_gain: float32 [2880], replicated, may hold values from 0.25 to 1.75
- router: float32 [2880, 8], replicated, may hold values from -0.21875 to 0.21875
- routes: int32 [2048, 4], P(('groups', 'att', 'exp')), parts along dimension 0, may hold values from 0 to 7, all different within a row; in each aligned block of 64 rows (0 to 63, 64 to 127, ...) at most 64 rows name the same one
- w_gate: bfloat16 [8, 2880, 1440], P('att', None, 'exp'), may hold values from -0.109375 to 0.109375
- w_up: bfloat16 [8, 2880, 1440], P('att', None, 'exp'), may hold values from -0.109375 to 0.109375
- w_down: bfloat16 [8, 1440, 2880], P('att', 'exp'), may hold values from -0.15625 to 0.15625
Outputs:
- mixed: bfloat16 [2048, 2880], P(('groups', 'att', 'exp')), parts along dimension 0
There are 2 independent parts, one for each index of `groups`. A program takes and returns all parts, laid end to end along the dimension named above; an argument that names none is the same for every part. Nothing has to cross between parts.
Inputs may be any that keep to these rules, and one draw needn't show every extreme that they name: `routes`: each row names 4 different experts. Among the 64 rows of one device (aligned blocks in order) no expert is named more than 64 times, and that count is reached in every draw. `lengths`: every eighth request, starting with the first, uses all 64 cached positions.
All inputs are finite; a program needn't handle non-finite values.
Results may differ from a plain program's by a relative error of at most 0.0065.
Values may be sent and summed in bfloat16 or wider, within the bound.
A program may use at most 128 MiB of HBM per device.

v0:
```python
import math
import jax
import jax.numpy as jnp
from jax import lax
from jax.sharding import PartitionSpec as P

HEAD = 64


def attend(query, new_key, new_value, cache_keys, cache_values, lengths):
    requests = query.shape[0]
    cache_len = cache_keys.shape[1]
    value_heads = new_key.shape[1] // HEAD
    group_size = query.shape[1] // new_key.shape[1]
    inverse_root = 1.0 / math.sqrt(HEAD)
    queries = query.reshape(requests, value_heads, group_size, HEAD)
    cached_k = cache_keys.reshape(requests, cache_len, value_heads, HEAD)
    cached_v = cache_values.reshape(requests, cache_len, value_heads, HEAD)
    fresh_k = new_key.reshape(requests, value_heads, HEAD)
    fresh_v = new_value.astype(jnp.float32).reshape(requests, value_heads, HEAD)
    cached_scores = (
        jnp.einsum("rjgd,rljd->rjgl", queries, cached_k, preferred_element_type=jnp.float32)
        * inverse_root
    )
    fresh_scores = (
        jnp.einsum("rjgd,rjd->rjg", queries, fresh_k, preferred_element_type=jnp.float32)
        * inverse_root
    )
    live_mask = jnp.arange(cache_len)[None, :] < lengths[:, None]
    cached_scores = jnp.where(live_mask[:, None, None, :], cached_scores, -1e30)
    highest = jnp.maximum(jnp.max(cached_scores, axis=-1), fresh_scores)
    cached_exp = jnp.exp(cached_scores - highest[..., None])
    fresh_exp = jnp.exp(fresh_scores - highest)
    totals = jnp.sum(cached_exp, axis=-1) + fresh_exp
    cached_probs = (cached_exp / totals[..., None]).astype(jnp.bfloat16)
    fresh_probs = (fresh_exp / totals).astype(jnp.bfloat16)
    output = jnp.einsum(
        "rjgl,rljd->rjgd", cached_probs, cached_v, preferred_element_type=jnp.float32
    )
    output = output + fresh_probs.astype(jnp.float32)[..., None] * fresh_v[:, :, None, :]
    return output.astype(jnp.bfloat16).reshape(requests, query.shape[1])


def per_device(
    query,
    new_key,
    new_value,
    cache_keys,
    cache_values,
    lengths,
    out_proj,
    residual,
    norm_gain,
    router,
    routes,
    w_gate,
    w_up,
    w_down,
):
    attended = attend(query, new_key, new_value, cache_keys, cache_values, lengths)
    summed = lax.psum_scatter(
        jnp.dot(attended, out_proj, preferred_element_type=jnp.float32),
        "exp",
        scatter_dimension=0,
        tiled=True,
    )
    hidden_state = residual.astype(jnp.float32) + summed
    mean_square = jnp.mean(hidden_state * hidden_state, axis=-1, keepdims=True)
    normed = (hidden_state * lax.rsqrt(mean_square + 1e-05) * norm_gain).astype(jnp.bfloat16)
    logits = jnp.dot(normed.astype(jnp.float32), router, precision=lax.Precision.HIGHEST)
    chosen_logits = jnp.take_along_axis(logits, routes, axis=1)
    squashed = jax.nn.sigmoid(chosen_logits)
    gate_weights = squashed / jnp.sum(squashed, axis=1, keepdims=True)
    experts = lax.axis_size("att")
    own_rows = routes.shape[0]
    top_count = routes.shape[1]
    width = normed.shape[1]
    capacity = 2 * own_rows * top_count // experts
    flat_routes = routes.reshape(-1)
    onehot = (flat_routes[:, None] == jnp.arange(experts)[None, :]).astype(jnp.int32)
    before = jnp.cumsum(onehot, axis=0) - onehot
    slot_index = jnp.sum(before * onehot, axis=1)
    target = flat_routes * capacity + slot_index
    placing = (jnp.arange(experts * capacity)[:, None] == target[None, :]).reshape(
        experts * capacity, own_rows, top_count
    )
    placing = jnp.any(placing, axis=2).astype(jnp.bfloat16)
    outgoing = jnp.dot(placing, normed, preferred_element_type=jnp.float32).astype(jnp.bfloat16)
    outgoing = outgoing.reshape(experts, capacity, width)
    gate_matrix = w_gate[0]
    up_matrix = w_up[0]
    down_matrix = w_down[0]
    arrived = lax.all_to_all(outgoing, "att", split_axis=0, concat_axis=0, tiled=True)
    routed_block = lax.all_gather(arrived, "exp", axis=1, tiled=True)
    leading = routed_block.shape[:-1]
    flat_rows = routed_block.reshape(-1, routed_block.shape[-1])
    gate_part = jnp.dot(flat_rows, gate_matrix, preferred_element_type=jnp.float32)
    up_part = jnp.dot(flat_rows, up_matrix, preferred_element_type=jnp.float32)
    activated = (jax.nn.silu(gate_part) * up_part).astype(jnp.bfloat16)
    result = jnp.dot(activated, down_matrix, preferred_element_type=jnp.float32)
    partial_value = result.reshape(leading + (result.shape[-1],))
    partial_value = lax.optimization_barrier(partial_value.astype(jnp.bfloat16)).astype(jnp.float32)
    summed_all = lax.psum(partial_value.astype(jnp.bfloat16), "exp").astype(jnp.float32)
    own_block = lax.dynamic_slice_in_dim(summed_all, lax.axis_index("exp") * capacity, capacity, 1)
    finished = own_block.astype(jnp.bfloat16)
    returned = lax.all_to_all(finished, "att", split_axis=0, concat_axis=0, tiled=True)
    flat_back = returned.reshape(-1, returned.shape[-1])
    picked = jnp.take(flat_back, target, axis=0).astype(jnp.float32)
    picked = picked.reshape(own_rows, top_count, returned.shape[-1])
    combined = jnp.sum(picked * gate_weights[:, :, None], axis=1)
    return (hidden_state + combined).astype(jnp.bfloat16)


def solution(mesh):
    in_specs = (
        P(("groups", "att"), "exp"),
        P(("groups", "att"), "exp"),
        P(("groups", "att"), "exp"),
        P(("groups", "att"), None, "exp"),
        P(("groups", "att"), None, "exp"),
        P(("groups", "att")),
        P("exp", None),
        P(("groups", "att", "exp"), None),
        P(),
        P(),
        P(("groups", "att", "exp"), None),
        P("att", None, "exp"),
        P("att", None, "exp"),
        P("att", "exp", None),
    )
    out_specs = P(("groups", "att", "exp"), None)
    return jax.shard_map(
        per_device, mesh=mesh, in_specs=in_specs, out_specs=out_specs, check_vma=False
    )
```

profile of v0, /device:TPU:0, one launch (start us, length us, event | category | flops | bytes accessed | tf_op | source)
XLA Modules:
  0.0 298.4 jit_solution(6635247010307698709)
XLA Ops:
  6.5 3.3 %copy.118 = bf16[128,64,128]{0,2,1:T(8,128)(2,1)S(1)} copy(bf16[128,64,128]{2,1,0:T(8,128)(2,1)} %param.18) | data formatting | bytes 4194304 | tf_op args[4]
  9.9 6.5 %copy.119 = bf16[128,64,2,64]{3,1,2,0:T(8,128)(2,1)} copy(bf16[128,64,2,64]{0,3,2,1:T(8,128)(2,1)S(1)} %bitcast.61) | data formatting | bytes 4194304 | tf_op jit(solution)/shard_map/reshape | solution.py:18
  16.4 0.2 copy.109
  16.5 0.4 copy.111
  17.0 3.3 %copy.110 = bf16[128,64,128]{0,2,1:T(8,128)(2,1)S(1)} copy(bf16[128,64,128]{2,1,0:T(8,128)(2,1)} %param.17) | data formatting | bytes 4194304 | tf_op args[3]
  20.3 6.5 %copy.112 = bf16[128,64,2,64]{3,1,2,0:T(8,128)(2,1)} copy(bf16[128,64,2,64]{0,3,2,1:T(8,128)(2,1)S(1)} %bitcast.62) | data formatting | bytes 4194304 | tf_op jit(solution)/shard_map/reshape | solution.py:17
  26.8 0.1 iota_compare_fusion.1
  26.9 0.1 copy.121
  27.0 0.1 copy.122
  27.2 4.6 %fusion.25 = (f32[128,2,8]{2,1,0:T(2,128)S(1)}, f32[128,2,8,64]{3,2,1,0:T(8,128)S(1)}) fusion(bf16[128,2,8,64]{3,2,1,0:T(8,128)(2,1)S(1)} %copy.111, bf16[128,64,2,64]{3,1,2,0:T(8,128)(2,1)} %copy.112, pred[128,64]{1,0:T(8,128)(4,1)S(1)} %iota_compare_fusion.1), kind=kOutput, calls=%fused_computation.57 | convolution fusion | flops 17168384 | bytes 2899968 | tf_op jit(solution)/shard_map/rjgd,rljd->rjgl/dot_general | solution.py:22
  31.8 0.1 copy.114
  31.9 0.1 copy.113
  32.0 0.1 multiply_reduce_fusion.2
  32.1 0.1 copy.115
  32.3 0.8 fusion.14
  33.0 0.1 copy.116
  33.1 0.2 copy.120
  33.3 0.1 copy.117
  33.4 3.5 %fusion.13 = bf16[128,2,8,64]{3,2,1,0:T(8,128)(2,1)S(1)} fusion(bf16[128,64,2,64]{3,1,2,0:T(8,128)(2,1)} %copy.119, f32[128,2,8,64]{3,2,1,0:T(8,128)S(1)} %get-tuple-element.10, f32[128,2,64]{2,1,0:T(2,128)S(1)} %copy.122, f32[128,2,8]{2,1,0:T(2,128)S(1)} %copy.120, f32[128,2,8]{2,1,0:T(2,128)S(1)} %copy.117, f32[128,2,8]{2,1,0:T(2,128)S(1)} %copy.115), kind=kOutput, calls=%fused_computation.18 | convolution fusion | flops 17563648 | bytes 2973696 | tf_op jit(solution)/shard_map/rjgl,rljd->rjgd/dot_general | solution.py:37
  37.0 0.5 copy.123
  37.5 6.0 %fusion.26 = f32[128,2880]{1,0:T(8,128)} fusion(bf16[128,1024]{0,1:T(8,128)(2,1)S(1)} %bitcast.64, bf16[1024,2880]{0,1:T(8,128)(2,1)} %param.20), kind=kOutput, calls=%fused_computation.58 | convolution fusion | flops 754974720 | bytes 7634944 | tf_op jit(solution)/shard_map/dot_general | solution.py:62
  43.5 0.0 reduce-scatter.2.cloned.1.call-update
  43.6 0.2 all-gather.2.cloned.1.call-start
  43.8 0.1 copy.124
  43.9 0.1 eq.40
  44.0 0.1 reshape.164
  44.1 0.6 reduce-window.6
  44.7 0.2 slice_reduce_fusion
  45.0 0.1 fusion.19
  45.1 0.1 reduce_sum.51
  45.2 0.1 copy.126
  45.3 0.1 fusion.17
  45.4 10.0 %reduce-scatter.2.cloned.1.call-done = f32[64,2880]{1,0:T(8,128)} async-done(((f32[128,2880]{1,0:T(8,128)}), f32[64,2880]{1,0:T(8,128)}) %reduce-scatter.2.cloned.1.call-update) | async-done | bytes 737296 | tf_op jit(solution)/shard_map/reduce_scatter | solution.py:61
  55.4 1.3 multiply_reduce_fusion.1
  56.8 1.3 multiply_convert_fusion.1
  58.0 1.0 convolution_convert_fusion.1
  59.0 3.0 copy.128
  62.0 74.5 %all_to_all.10 = bf16[8,64,2880]{2,1,0:T(8,128)(2,1)} all-to-all(bf16[8,64,2880]{2,1,0:T(8,128)(2,1)} %bitcast.60), channel_id=1, replica_groups=mesh['groups'=2,'att'=8,'exp'=2] {'att'}, dimensions={0} | all-to-all | bytes 5898240 | tf_op jit(solution)/shard_map/all_to_all | solution.py:93
  136.5 0.0 all-gather.2.cloned.1.call-update
  136.6 0.0 all-reduce.2.cloned.1.call-start
  136.6 15.1 %all-gather.2.cloned.1.call-done = bf16[8,128,2880]{2,1,0:T(8,128)(2,1)} async-done(((bf16[8,64,2880]{2,1,0:T(8,128)(2,1)}), bf16[8,128,2880]{2,1,0:T(8,128)(2,1)}) %all-gather.2.cloned.1.call-update) | async-done | bytes 5898256 | tf_op jit(solution)/shard_map/all_gather | solution.py:94
  151.8 8.2 %fusion.1 = f32[1024,720]{0,1:T(8,128)S(1)} fusion(bf16[1024,2880]{1,0:T(8,128)(2,1)} %bitcast.68, bf16[1,2880,720]{1,2,0:T(8,128)(2,1)} %param.26), kind=kOutput, calls=%fused_computation.6 | convolution fusion | flops 4246732800 | bytes 12994560 | tf_op jit(solution)/shard_map/dot_general | solution.py:98
  160.0 0.0 slice-start.3
  160.0 5.2 %fusion.9 = bf16[90,8,8,128]{3,2,1,0:T(8,128)(2,1)S(1)} fusion(f32[1024,720]{0,1:T(8,128)S(1)} %fusion.1, bf16[1024,2880]{1,0:T(8,128)(2,1)S(1)} %bitcast.69, bf16[1,2880,720]{1,2,0:T(8,128)(2,1)S(1)} %bitcast.71), kind=kOutput, calls=%fused_computation.14 | convolution fusion | flops 4251156480 | bytes 14469120 | tf_op jit(solution)/shard_map/dot_general | solution.py:97
  165.3 7.1 %convolution_convert_fusion = bf16[8,128,2880]{2,1,0:T(8,128)(2,1)} fusion(bf16[1,720,2880]{2,1,0:T(8,128)(2,1)S(1)} %bitcast.73, bf16[90,8,8,128]{3,2,1,0:T(8,128)(2,1)S(1)} %fusion.9), kind=kOutput, calls=%fused_computation.3 | convolution fusion | flops 4249681920 | bytes 11520000 | tf_op jit(solution)/shard_map/dot_general | solution.py:100
  172.4 0.0 all-reduce.2.cloned.1.call-update
  172.4 32.2 %all-reduce.2.cloned.1.call-done = bf16[8,128,2880]{2,1,0:T(8,128)(2,1)} async-done(((bf16[8,128,2880]{2,1,0:T(8,128)(2,1)}), bf16[8,128,2880]{2,1,0:T(8,128)(2,1)}) %all-reduce.2.cloned.1.call-update) | async-done | bytes 5898256 | tf_op jit(solution)/shard_map/psum | solution.py:103
  204.6 3.7 %convert_convert_fusion = bf16[8,64,2880]{2,1,0:T(8,128)(2,1)} fusion(bf16[8,128,2880]{2,1,0:T(8,128)(2,1)} %all-reduce.2.cloned.1.call-done, s32[]{:T(128)S(6)} %select_n.41), kind=kLoop, calls=%fused_computation.2 | loop fusion | flops 2949120 | bytes 5898244 | tf_op jit(solution)/shard_map/convert_element_type | solution.py:105
  208.3 5.8 %all-to-all-start.1 = ((bf16[8,64,2880]{2,1,0:T(8,128)(2,1)}), bf16[8,64,2880]{2,1,0:T(8,128)(2,1)S(1)}, u32[]{:S(2)}, u32[]{:S(2)}) async-start(bf16[8,64,2880]{2,1,0:T(8,128)(2,1)} %convert_convert_fusion), calls=%async_computation.2 | async-start | bytes 6029312 | tf_op jit(solution)/shard_map/all_to_all | solution.py:106
  214.1 0.1 copy.132
  214.2 0.1 reshape.179
  214.3 0.1 copy.131
  214.4 0.1 mul.113
  214.5 0.1 copy.127
  214.7 0.4 fusion.27
  215.1 1.5 gather_fusion.1
  216.5 0.1 reshape.182
  216.6 0.1 copy.133
  216.8 0.1 copy.134
  216.9 65.6 %all-to-all-done.1 = bf16[8,64,2880]{2,1,0:T(8,128)(2,1)S(1)} async-done(((bf16[8,64,2880]{2,1,0:T(8,128)(2,1)}), bf16[8,64,2880]{2,1,0:T(8,128)(2,1)S(1)}, u32[]{:S(2)}, u32[]{:S(2)}) %all-to-all-start.1) | async-done | bytes 2949152 | tf_op jit(solution)/shard_map/all_to_all | solution.py:106
  282.4 2.7 gather_fusion
  285.1 2.9 gather.11
  288.0 3.0 %multiply_reduce_fusion = f32[64,2880]{1,0:T(8,128)S(1)} fusion(f32[64,4]{1,0:T(8,128)S(1)} %copy.134, bf16[64,4,2880]{2,1,0:T(4,128)(2,1)S(1)} %gather.11, pred[64,4]{1,0:T(8,128)(4,1)S(1)} %copy.127), kind=kLoop, calls=%fused_computation.10 | loop fusion | flops 2764800 | bytes 2213120 | tf_op jit(solution)/shard_map/reduce_sum | solution.py:110
  291.1 0.8 add_convert_fusion
  (46 shorter events, 0.3 us)
Async XLA Ops:
  6.5 208.1 %copy-start = (f32[2880,8]{0,1:T(8,128)S(1)}, f32[2880,8]{0,1:T(8,128)}, u32[]{:S(2)}) copy-start(f32[2880,8]{0,1:T(8,128)} %param.23) | copy-start | bytes 276484
  6.5 48.9 %reduce-scatter.2.cloned.1.call-start = ((), (), s32[]{:S(2)}) async-start(), calls=%async_computation.3 | async-start | bytes 2260992 | tf_op jit(solution)/shard_map/reduce_scatter | solution.py:61
  9.9 6.5 %copy-start.4 = (bf16[128,1024]{1,0:T(8,128)(2,1)S(1)}, bf16[128,1024]{1,0:T(8,128)(2,1)}, u32[]{:S(2)}) copy-start(bf16[128,1024]{1,0:T(8,128)(2,1)} %param.14) | copy-start | bytes 786436
  20.3 6.5 %copy-start.9 = (s32[128]{0:T(128)S(1)}, s32[128]{0:T(128)}, u32[]{:S(2)}) copy-start(s32[128]{0:T(128)} %param.19) | copy-start | bytes 1540
  20.3 6.6 %copy-start.6 = (bf16[128,128]{1,0:T(8,128)(2,1)S(1)}, bf16[128,128]{1,0:T(8,128)(2,1)}, u32[]{:S(2)}) copy-start(bf16[128,128]{1,0:T(8,128)(2,1)} %param.16) | copy-start | bytes 98308
  27.2 4.7 %copy-start.7 = (bf16[128,128]{1,0:T(8,128)(2,1)S(1)}, bf16[128,128]{1,0:T(8,128)(2,1)}, u32[]{:S(2)}) copy-start(bf16[128,128]{1,0:T(8,128)(2,1)} %param.15) | copy-start | bytes 98308
  37.5 6.3 %copy-start.5 = (s32[64,4]{0,1:T(4,128)S(1)}, s32[64,4]{0,1:T(4,128)}, u32[]{:S(2)}) copy-start(s32[64,4]{0,1:T(4,128)} %param.24) | copy-start | bytes 3076
  37.5 17.9 %copy-start.2 = (bf16[64,2880]{1,0:T(8,128)(2,1)S(1)}, bf16[64,2880]{1,0:T(8,128)(2,1)}, u32[]{:S(2)}) copy-start(bf16[64,2880]{1,0:T(8,128)(2,1)} %param.21) | copy-start | bytes 1105924
  37.5 19.3 %copy-start.8 = (f32[2880]{0:T(1024)S(1)}, f32[2880]{0:T(1024)}, u32[]{:S(2)}) copy-start(f32[2880]{0:T(1024)} %param.22) | copy-start | bytes 34564
  43.6 108.2 %all-gather.2.cloned.1.call-start = ((), (), s32[]{:S(2)}) async-start(), calls=%async_computation.4 | async-start | bytes 9043968 | tf_op jit(solution)/shard_map/all_gather | solution.py:94
  136.5 23.5 %slice-start = ((s8[4239360]{0:T(1024)(128)(4,1)}), s8[45056]{0:T(1024)(128)(4,1)S(1)}, s32[]{:S(2)}) async-start(s8[4239360]{0:T(1024)(128)(4,1)} %bitcast.70), calls=%async_computation.6 | async-start | bytes 90112
  136.6 68.0 %all-reduce.2.cloned.1.call-start = ((), (), s32[]{:S(2)}) async-start(), calls=%async_computation.5 | async-start | bytes 12058624 | tf_op jit(solution)/shard_map/psum | solution.py:103
  151.8 8.3 %copy-start.10 = (bf16[8,128,2880]{2,1,0:T(8,128)(2,1)S(1)}, bf16[8,128,2880]{2,1,0:T(8,128)(2,1)}, u32[]{:S(2)}) copy-start(bf16[8,128,2880]{2,1,0:T(8,128)(2,1)} %all-gather.2.cloned.1.call-done) | copy-start | bytes 17694724
  151.8 8.3 %slice-start.1 = ((s8[4239360]{0:T(1024)(128)(4,1)}), s8[4194304]{0:T(1024)(128)(4,1)S(1)}, s32[]{:S(2)}) async-start(s8[4239360]{0:T(1024)(128)(4,1)} %bitcast.70), calls=%async_computation.7 | async-start | bytes 8388608
  151.8 13.5 %slice-start.2 = ((s8[4239360]{0:T(1024)(128)(4,1)}), s8[4194304]{0:T(1024)(128)(4,1)S(1)}, s32[]{:S(2)}) async-start(s8[4239360]{0:T(1024)(128)(4,1)} %bitcast.72), calls=%async_computation.8 | async-start | bytes 8388608
  160.0 5.2 %slice-start.3 = ((s8[4239360]{0:T(1024)(128)(4,1)}), s8[45056]{0:T(1024)(128)(4,1)S(1)}, s32[]{:S(2)}) async-start(s8[4239360]{0:T(1024)(128)(4,1)} %bitcast.72), calls=%async_computation.9 | async-start | bytes 90112
  208.3 74.1 %all-to-all-start.1 = ((bf16[8,64,2880]{2,1,0:T(8,128)(2,1)}), bf16[8,64,2880]{2,1,0:T(8,128)(2,1)S(1)}, u32[]{:S(2)}, u32[]{:S(2)}) async-start(bf16[8,64,2880]{2,1,0:T(8,128)(2,1)} %convert_convert_fusion), calls=%async_computation.2 | async-start | bytes 6029312 | tf_op jit(solution)/shard_map/all_to_all | solution.py:106
  285.1 5.9 %copy-start.1 = (f32[64,2880]{1,0:T(8,128)S(1)}, f32[64,2880]{1,0:T(8,128)}, u32[]{:S(2)}) copy-start(f32[64,2880]{1,0:T(8,128)} %reduce-scatter.2.cloned.1.call-done) | copy-start | bytes 2211844
  285.1 5.9 %copy-start.3 = (bf16[64,2880]{1,0:T(8,128)(2,1)S(1)}, bf16[64,2880]{1,0:T(8,128)(2,1)}, u32[]{:S(2)}) copy-start(bf16[64,2880]{1,0:T(8,128)(2,1)} %param.21) | copy-start | bytes 1105924
Sparse Core Ops, SparseCore 0:
  43.7 11.6 reduce-scatter.1
  136.7 15.0 all-gather.1
  172.5 31.9 all-reduce.1
where the time goes:
time: 299 us; the launch traced here: 298 us
  waiting for transfers between devices  123 us (41%)
  blocking collectives  74.5 us (25%)
  matrix products  36.1 us (12%)
  local copies, waits for them, and re-layouts  33.2 us (11%)
  between operations  13.6 us (5%)
  other arithmetic  12.1 us (4%)
  starting transfers between devices  6.05 us (2%)
    all_to_all x1, blocking collectives, per_device(): lax.all_to_all(outgoing, 'att', split_axis=0, concat_axis=0, tiled=True)  74.5 us
    all_to_all x1, waiting for transfers between devices, per_device(): lax.all_to_all(finished, 'att', split_axis=0, concat_axis=0, tiled=True)  65.6 us
    psum x1, waiting for transfers between devices, per_device(): lax.psum(partial_value.astype(jnp.bfloat16), 'exp').astype(jnp.float32)  32.2 us
    all_gather x1, waiting for transfers between devices, per_device(): routed_block = lax.all_gather(arrived, 'exp', axis=1, tiled=True)  15.1 us
    reduce_scatter x1, waiting for transfers between devices, per_device(): lax.psum_scatter(jnp.dot(attended, out_proj, preferred_element_type=jnp.f...  10 us
    dot_general x1, matrix products, per_device(): up_part = jnp.dot(flat_rows, up_matrix, preferred_element_type=jnp.float32)  8.23 us
    unnamed x36, local copies, waits for them, and re-layouts  7.23 us
    dot_general x1, matrix products, per_device(): result = jnp.dot(activated, down_matrix, preferred_element_type=jnp.float32)  7.08 us
  transfers between devices with their start and end apart: 4, of which 4 were waited for; matrix products, arithmetic and copies ran while one was open for 1% of the time, Pallas kernels for 0%

commit v1 on v0

--- a/solution.py
+++ b/solution.py
@@ -5,6 +5,11 @@
 from jax.sharding import PartitionSpec as P
 
 HEAD = 64
+
+
+def add_all(shard, axis):
+    blocks = lax.all_gather(shard, axis)
+    return jnp.sum(blocks, axis=0)
 
 
 def attend(query, new_key, new_value, cache_keys, cache_values, lengths):
@@ -100,7 +105,7 @@
     result = jnp.dot(activated, down_matrix, preferred_element_type=jnp.float32)
     partial_value = result.reshape(leading + (result.shape[-1],))
     partial_value = lax.optimization_barrier(partial_value.astype(jnp.bfloat16)).astype(jnp.float32)
-    summed_all = lax.psum(partial_value.astype(jnp.bfloat16), "exp").astype(jnp.float32)
+    summed_all = add_all(partial_value.astype(jnp.bfloat16), "exp").astype(jnp.float32)
     own_block = lax.dynamic_slice_in_dim(summed_all, lax.axis_index("exp") * capacity, capacity, 1)
     finished = own_block.astype(jnp.bfloat16)
     returned = lax.all_to_all(finished, "att", split_axis=0, concat_axis=0, tiled=True)

time: 299 us -> 313 us (1.047)
  local copies, waits for them, and re-layouts: 33.2 us -> 45.3 us
  other arithmetic: 12.1 us -> 21.2 us
  waiting for transfers between devices: 123 us -> 116 us
    psum x1 -> x0, waiting for transfers between devices: 32.2 us -> none  [per_device(): lax.psum(partial_value.astype(jnp.bfloat16), 'exp').astype(jnp.float32)]
    all_gather x0 -> x1, waiting for transfers between devices: none -> 25.2 us  [add_all(): blocks = lax.all_gather(shard, axis)]
    reduce_sum x0 -> x1, other arithmetic: none -> 11 us  [add_all(): return jnp.sum(blocks, axis=0)]
    dynamic_slice x0 -> x1, local copies, waits for them, and re-layouts: none -> 6.82 us  [per_device(): lax.dynamic_slice_in_dim(summed_all, lax.axis_index('exp') * capacity, ca...]
    unnamed x36 -> x37, local copies, waits for them, and re-layouts: 7.23 us -> 12.6 us
where the time goes in v1:
time: 313 us; the launch traced here: 312 us
  waiting for transfers between devices  116 us (37%)
  blocking collectives  74.5 us (24%)
  local copies, waits for them, and re-layouts  45.3 us (14%)
  matrix products  35.8 us (11%)
  other arithmetic  21.2 us (7%)
  between operations  13.6 us (4%)
  starting transfers between devices  6.05 us (2%)
    all_to_all x1, blocking collectives, per_device(): lax.all_to_all(outgoing, 'att', split_axis=0, concat_axis=0, tiled=True)  74.5 us
    all_to_all x1, waiting for transfers between devices, per_device(): lax.all_to_all(finished, 'att', split_axis=0, concat_axis=0, tiled=True)  65.6 us
    all_gather x1, waiting for transfers between devices, add_all(): blocks = lax.all_gather(shard, axis)  25.2 us
    all_gather x1, waiting for transfers between devices, per_device(): routed_block = lax.all_gather(arrived, 'exp', axis=1, tiled=True)  15.1 us
    unnamed x37, local copies, waits for them, and re-layouts  12.6 us
    reduce_sum x1, other arithmetic, add_all(): return jnp.sum(blocks, axis=0)  11 us
    reduce_scatter x1, waiting for transfers between devices, per_device(): lax.psum_scatter(jnp.dot(attended, out_proj, preferred_element_type=jnp.f...  10 us
    dot_general x1, matrix products, per_device(): up_part = jnp.dot(flat_rows, up_matrix, preferred_element_type=jnp.float32)  8.23 us
  transfers between devices with their start and end apart: 4, of which 4 were waited for; matrix products, arithmetic and copies ran while one was open for 1% of the time, Pallas kernels for 0%

profile of v1, /device:TPU:0, one launch (start us, length us, event | category | flops | bytes accessed | tf_op | source)
XLA Modules:
  0.0 312.5 jit_solution(11227837468834344853)
XLA Ops:
  6.5 3.3 %copy.138 = bf16[128,64,128]{0,2,1:T(8,128)(2,1)S(1)} copy(bf16[128,64,128]{2,1,0:T(8,128)(2,1)} %param.18) | data formatting | bytes 4194304 | tf_op args[4]
  9.9 6.5 %copy.139 = bf16[128,64,2,64]{3,1,2,0:T(8,128)(2,1)} copy(bf16[128,64,2,64]{0,3,2,1:T(8,128)(2,1)S(1)} %bitcast.63) | data formatting | bytes 4194304 | tf_op jit(solution)/shard_map/reshape | solution.py:23
  16.4 0.2 copy.129
  16.5 0.4 copy.131
  17.0 3.3 %copy.130 = bf16[128,64,128]{0,2,1:T(8,128)(2,1)S(1)} copy(bf16[128,64,128]{2,1,0:T(8,128)(2,1)} %param.17) | data formatting | bytes 4194304 | tf_op args[3]
  20.3 6.5 %copy.132 = bf16[128,64,2,64]{3,1,2,0:T(8,128)(2,1)} copy(bf16[128,64,2,64]{0,3,2,1:T(8,128)(2,1)S(1)} %bitcast.64) | data formatting | bytes 4194304 | tf_op jit(solution)/shard_map/reshape | solution.py:22
  26.8 0.1 iota_compare_fusion.1
  26.9 0.1 copy.141
  27.0 0.1 copy.142
  27.2 4.6 %fusion.25 = (f32[128,2,8]{2,1,0:T(2,128)S(1)}, f32[128,2,8,64]{3,2,1,0:T(8,128)S(1)}) fusion(bf16[128,2,8,64]{3,2,1,0:T(8,128)(2,1)S(1)} %copy.131, bf16[128,64,2,64]{3,1,2,0:T(8,128)(2,1)} %copy.132, pred[128,64]{1,0:T(8,128)(4,1)S(1)} %iota_compare_fusion.1), kind=kOutput, calls=%fused_computation.58 | convolution fusion | flops 17168384 | bytes 2899968 | tf_op jit(solution)/shard_map/rjgd,rljd->rjgl/dot_general | solution.py:27
  31.8 0.1 copy.134
  31.9 0.1 copy.133
  32.0 0.1 multiply_reduce_fusion.2
  32.1 0.1 copy.135
  32.3 0.8 fusion.14
  33.0 0.1 copy.136
  33.1 0.2 copy.140
  33.3 0.1 copy.137
  33.4 3.5 %fusion.13 = bf16[128,2,8,64]{3,2,1,0:T(8,128)(2,1)S(1)} fusion(bf16[128,64,2,64]{3,1,2,0:T(8,128)(2,1)} %copy.139, f32[128,2,8,64]{3,2,1,0:T(8,128)S(1)} %get-tuple-element.10, f32[128,2,64]{2,1,0:T(2,128)S(1)} %copy.142, f32[128,2,8]{2,1,0:T(2,128)S(1)} %copy.140, f32[128,2,8]{2,1,0:T(2,128)S(1)} %copy.137, f32[128,2,8]{2,1,0:T(2,128)S(1)} %copy.135), kind=kOutput, calls=%fused_computation.18 | convolution fusion | flops 17563648 | bytes 2973696 | tf_op jit(solution)/shard_map/rjgl,rljd->rjgd/dot_general | solution.py:42
  37.0 0.5 copy.143
  37.5 6.0 %fusion.26 = f32[128,2880]{1,0:T(8,128)} fusion(bf16[128,1024]{0,1:T(8,128)(2,1)S(1)} %bitcast.66, bf16[1024,2880]{0,1:T(8,128)(2,1)} %param.20), kind=kOutput, calls=%fused_computation.59 | convolution fusion | flops 754974720 | bytes 7634944 | tf_op jit(solution)/shard_map/dot_general | solution.py:67
  43.6 0.2 all-gather.4.cloned.1.call-start
  43.8 0.1 copy.144
  43.9 0.1 eq.40
  44.0 0.1 reshape.164
  44.1 0.6 reduce-window.6
  44.7 0.2 slice_reduce_fusion
  45.0 0.1 fusion.19
  45.1 0.1 reduce_sum.63
  45.2 0.1 copy.146
  45.3 0.1 fusion.17
  45.4 10.0 %reduce-scatter.2.cloned.1.call-done = f32[64,2880]{1,0:T(8,128)} async-done(((f32[128,2880]{1,0:T(8,128)}), f32[64,2880]{1,0:T(8,128)}) %reduce-scatter.2.cloned.1.call-update) | async-done | bytes 737296 | tf_op jit(solution)/shard_map/reduce_scatter | solution.py:66
  55.4 1.3 multiply_reduce_fusion.1
  56.8 1.3 multiply_convert_fusion.1
  58.0 1.0 convolution_convert_fusion.1
  59.0 3.0 copy.148
  62.0 74.5 %all_to_all.10 = bf16[8,64,2880]{2,1,0:T(8,128)(2,1)} all-to-all(bf16[8,64,2880]{2,1,0:T(8,128)(2,1)} %bitcast.61), channel_id=1, replica_groups=mesh['groups'=2,'att'=8,'exp'=2] {'att'}, dimensions={0} | all-to-all | bytes 5898240 | tf_op jit(solution)/shard_map/all_to_all | solution.py:98
  136.5 0.0 all-gather.4.cloned.1.call-update
  136.6 0.0 all-gather.6.cloned.1.call-start
  136.6 15.1 %all-gather.4.cloned.1.call-done = bf16[8,128,2880]{2,1,0:T(8,128)(2,1)} async-done(((bf16[8,64,2880]{2,1,0:T(8,128)(2,1)}), bf16[8,128,2880]{2,1,0:T(8,128)(2,1)}) %all-gather.4.cloned.1.call-update) | async-done | bytes 5898256 | tf_op jit(solution)/shard_map/all_gather | solution.py:99
  151.8 8.2 %fusion.1 = f32[1024,720]{0,1:T(8,128)S(1)} fusion(bf16[1024,2880]{1,0:T(8,128)(2,1)} %bitcast.70, bf16[1,2880,720]{1,2,0:T(8,128)(2,1)} %param.26), kind=kOutput, calls=%fused_computation.6 | convolution fusion | flops 4246732800 | bytes 12994560 | tf_op jit(solution)/shard_map/dot_general | solution.py:103
  160.0 5.2 %fusion.9 = bf16[90,8,8,128]{3,2,1,0:T(8,128)(2,1)S(1)} fusion(f32[1024,720]{0,1:T(8,128)S(1)} %fusion.1, bf16[1024,2880]{1,0:T(8,128)(2,1)S(1)} %bitcast.71, bf16[1,2880,720]{1,2,0:T(8,128)(2,1)S(1)} %bitcast.73), kind=kOutput, calls=%fused_computation.14 | convolution fusion | flops 4251156480 | bytes 14469120 | tf_op jit(solution)/shard_map/dot_general | solution.py:102
  165.3 6.8 %convolution_convert_fusion = bf16[8,128,2880]{1,2,0:T(8,128)(2,1)} fusion(bf16[1,720,2880]{2,1,0:T(8,128)(2,1)S(1)} %bitcast.75, bf16[90,8,8,128]{3,2,1,0:T(8,128)(2,1)S(1)} %fusion.9), kind=kOutput, calls=%fused_computation.3 | convolution fusion | flops 4249681920 | bytes 11520000 | tf_op jit(solution)/shard_map/dot_general | solution.py:105
  172.1 25.2 %all-gather.6.cloned.1.call-done = bf16[16,128,2880]{1,2,0:T(8,128)(2,1)} async-done(((bf16[8,128,2880]{1,2,0:T(8,128)(2,1)}), bf16[16,128,2880]{1,2,0:T(8,128)(2,1)}) %all-gather.6.cloned.1.call-update) | async-done | bytes 11796496 | tf_op jit(solution)/shard_map/all_gather | solution.py:11
  197.3 11.0 %reduce_sum.65 = bf16[8,128,2880]{1,2,0:T(8,128)(2,1)} reduce(bf16[2,8,128,2880]{2,3,1,0:T(8,128)(2,1)} %bitcast.62, bf16[]{:T(256)} %constant.60.clone.1), dimensions={0}, to_apply=%region_8.9 | reduce | flops 2949120 | bytes 17694722 | tf_op jit(solution)/shard_map/reduce_sum | solution.py:12
  208.3 6.8 %constant_dynamic-slice_fusion = bf16[8,64,2880]{1,2,0:T(8,128)(2,1)} fusion(bf16[8,128,2880]{1,2,0:T(8,128)(2,1)} %reduce_sum.65, s32[]{:T(128)S(6)} %select_n.41), kind=kLoop, calls=%fused_computation.55 | loop fusion | bytes 5898244 | tf_op jit(solution)/shard_map/dynamic_slice | solution.py:109
  215.2 5.3 %copy.162 = bf16[8,64,2880]{2,1,0:T(8,128)(2,1)S(1)} copy(bf16[8,64,2880]{1,2,0:T(8,128)(2,1)} %constant_dynamic-slice_fusion) | data formatting | bytes 5898240
  220.5 1.9 convert_convert_fusion
  222.4 5.8 %all-to-all-start.1 = ((bf16[8,64,2880]{2,1,0:T(8,128)(2,1)}), bf16[8,64,2880]{2,1,0:T(8,128)(2,1)S(1)}, u32[]{:S(2)}, u32[]{:S(2)}) async-start(bf16[8,64,2880]{2,1,0:T(8,128)(2,1)} %convert_convert_fusion), calls=%async_computation.2 | async-start | bytes 6029312 | tf_op jit(solution)/shard_map/all_to_all | solution.py:111
  228.2 0.1 copy.152
  228.3 0.1 reshape.179
  228.4 0.1 copy.151
  228.5 0.1 mul.113
  228.6 0.1 copy.147
  228.7 0.4 fusion.27
  229.1 1.5 gather_fusion.1
  230.6 0.1 reshape.182
  230.7 0.1 copy.153
  230.8 0.1 copy.154
  230.9 65.6 %all-to-all-done.1 = bf16[8,64,2880]{2,1,0:T(8,128)(2,1)S(1)} async-done(((bf16[8,64,2880]{2,1,0:T(8,128)(2,1)}), bf16[8,64,2880]{2,1,0:T(8,128)(2,1)S(1)}, u32[]{:S(2)}, u32[]{:S(2)}) %all-to-all-start.1) | async-done | bytes 2949152 | tf_op jit(solution)/shard_map/all_to_all | solution.py:111
  296.5 2.7 gather_fusion
  299.2 2.9 gather.11
  302.1 3.0 multiply_reduce_fusion
  305.1 0.8 add_convert_fusion
  (49 shorter events, 0.3 us)
Async XLA Ops:
  6.5 222.2 %copy-start = (f32[2880,8]{0,1:T(8,128)S(1)}, f32[2880,8]{0,1:T(8,128)}, u32[]{:S(2)}) copy-start(f32[2880,8]{0,1:T(8,128)} %param.23) | copy-start | bytes 276484
  6.5 48.9 %reduce-scatter.2.cloned.1.call-start = ((), (), s32[]{:S(2)}) async-start(), calls=%async_computation.3 | async-start | bytes 2260992 | tf_op jit(solution)/shard_map/reduce_scatter | solution.py:66
  9.9 6.5 %copy-start.4 = (bf16[128,1024]{1,0:T(8,128)(2,1)S(1)}, bf16[128,1024]{1,0:T(8,128)(2,1)}, u32[]{:S(2)}) copy-start(bf16[128,1024]{1,0:T(8,128)(2,1)} %param.14) | copy-start | bytes 786436
  20.3 6.5 %copy-start.9 = (s32[128]{0:T(128)S(1)}, s32[128]{0:T(128)}, u32[]{:S(2)}) copy-start(s32[128]{0:T(128)} %param.19) | copy-start | bytes 1540
  20.3 6.6 %copy-start.6 = (bf16[128,128]{1,0:T(8,128)(2,1)S(1)}, bf16[128,128]{1,0:T(8,128)(2,1)}, u32[]{:S(2)}) copy-start(bf16[128,128]{1,0:T(8,128)(2,1)} %param.16) | copy-start | bytes 98308
  27.2 4.7 %copy-start.7 = (bf16[128,128]{1,0:T(8,128)(2,1)S(1)}, bf16[128,128]{1,0:T(8,128)(2,1)}, u32[]{:S(2)}) copy-start(bf16[128,128]{1,0:T(8,128)(2,1)} %param.15) | copy-start | bytes 98308
  37.5 6.3 %copy-start.5 = (s32[64,4]{0,1:T(4,128)S(1)}, s32[64,4]{0,1:T(4,128)}, u32[]{:S(2)}) copy-start(s32[64,4]{0,1:T(4,128)} %param.24) | copy-start | bytes 3076
  37.5 17.9 %copy-start.2 = (bf16[64,2880]{1,0:T(8,128)(2,1)S(1)}, bf16[64,2880]{1,0:T(8,128)(2,1)}, u32[]{:S(2)}) copy-start(bf16[64,2880]{1,0:T(8,128)(2,1)} %param.21) | copy-start | bytes 1105924
  37.5 19.3 %copy-start.8 = (f32[2880]{0:T(1024)S(1)}, f32[2880]{0:T(1024)}, u32[]{:S(2)}) copy-start(f32[2880]{0:T(1024)} %param.22) | copy-start | bytes 34564
  43.6 108.2 %all-gather.4.cloned.1.call-start = ((), (), s32[]{:S(2)}) async-start(), calls=%async_computation.4 | async-start | bytes 9043968 | tf_op jit(solution)/shard_map/all_gather | solution.py:99
  136.5 23.5 %slice-start = ((s8[4239360]{0:T(1024)(128)(4,1)}), s8[45056]{0:T(1024)(128)(4,1)S(1)}, s32[]{:S(2)}) async-start(s8[4239360]{0:T(1024)(128)(4,1)} %bitcast.72), calls=%async_computation.6 | async-start | bytes 90112
  136.6 60.8 %all-gather.6.cloned.1.call-start = ((), (), s32[]{:S(2)}) async-start(), calls=%async_computation.5 | async-start | bytes 17694720 | tf_op jit(solution)/shard_map/all_gather | solution.py:11
  151.8 8.3 %copy-start.10 = (bf16[8,128,2880]{2,1,0:T(8,128)(2,1)S(1)}, bf16[8,128,2880]{2,1,0:T(8,128)(2,1)}, u32[]{:S(2)}) copy-start(bf16[8,128,2880]{2,1,0:T(8,128)(2,1)} %all-gather.4.cloned.1.call-done) | copy-start | bytes 17694724
  151.8 8.3 %slice-start.1 = ((s8[4239360]{0:T(1024)(128)(4,1)}), s8[4194304]{0:T(1024)(128)(4,1)S(1)}, s32[]{:S(2)}) async-start(s8[4239360]{0:T(1024)(128)(4,1)} %bitcast.72), calls=%async_computation.7 | async-start | bytes 8388608
  151.8 13.5 %slice-start.2 = ((s8[4239360]{0:T(1024)(128)(4,1)}), s8[4194304]{0:T(1024)(128)(4,1)S(1)}, s32[]{:S(2)}) async-start(s8[4239360]{0:T(1024)(128)(4,1)} %bitcast.74), calls=%async_computation.8 | async-start | bytes 8388608
  160.0 5.2 %slice-start.3 = ((s8[4239360]{0:T(1024)(128)(4,1)}), s8[45056]{0:T(1024)(128)(4,1)S(1)}, s32[]{:S(2)}) async-start(s8[4239360]{0:T(1024)(128)(4,1)} %bitcast.74), calls=%async_computation.9 | async-start | bytes 90112
  222.4 74.1 %all-to-all-start.1 = ((bf16[8,64,2880]{2,1,0:T(8,128)(2,1)}), bf16[8,64,2880]{2,1,0:T(8,128)(2,1)S(1)}, u32[]{:S(2)}, u32[]{:S(2)}) async-start(bf16[8,64,2880]{2,1,0:T(8,128)(2,1)} %convert_convert_fusion), calls=%async_computation.2 | async-start | bytes 6029312 | tf_op jit(solution)/shard_map/all_to_all | solution.py:111
  299.2 5.9 %copy-start.1 = (f32[64,2880]{1,0:T(8,128)S(1)}, f32[64,2880]{1,0:T(8,128)}, u32[]{:S(2)}) copy-start(f32[64,2880]{1,0:T(8,128)} %reduce-scatter.2.cloned.1.call-done) | copy-start | bytes 2211844
  299.2 5.9 %copy-start.3 = (bf16[64,2880]{1,0:T(8,128)(2,1)S(1)}, bf16[64,2880]{1,0:T(8,128)(2,1)}, u32[]{:S(2)}) copy-start(bf16[64,2880]{1,0:T(8,128)(2,1)} %param.21) | copy-start | bytes 1105924
Sparse Core Ops, SparseCore 0:
  43.7 11.6 reduce-scatter.1
  136.7 15.0 all-gather.3
  172.2 25.0 all-gather.5
